TPU v7x, 512 devices: a whole 4x8x8 slice. The times are simulated.
512 devices in a mesh: cell: 128 (over z, y, core), pool: 4 (over x).
Axes of the slice: x: 4, y: 8, z: 8, core: 2. Of those that a mesh axis runs over, the one named last changes fastest.
Arguments:
- fractions: bfloat16 [256, 131072], P(None, 'cell'), may hold values from 0 to 1, as said below
- order: int32 [131072], P('cell'), may hold values from 0 to 131071, as said below
- density: float32 [8, 16, 131072], P('pool', None, 'cell'), may hold values from 0.2 to 5
- area: float32 [16, 131072], P(None, 'cell'), may hold values from 0.05 to 3
- harvest: float32 [8], P('pool'), may hold values from 0.05 to 0.6
Outputs:
- new_density: float32 [8, 16, 131072], P('pool', None, 'cell')
- area_cum: float32 [16, 131072], P(None, 'cell')
- stock_mean: float32 [8, 16], P('pool')
- removed: float32 [16], replicated
Inputs may be any that keep to these rules, and one draw needn't show every extreme that they name: A permutation of the cells; of the cells that one device holds in region order, every gridcell block of 1024 positions receives the same number. `fractions`: each column of a cell's matrix sums to one before rounding, with diagonal entries of 0.4 or more.
All inputs are finite; a program needn't handle non-finite values.
Results may differ from a plain program's by a relative error of at most 0.0003.
Values may be sent and summed in bfloat16 or wider, within the bound.
A program may use at most 64 MiB of HBM per device.

v0:
```python
import jax
import jax.numpy as jnp
from jax import lax
from jax.sharding import Mesh
from jax.sharding import PartitionSpec as P

CELL = ("cell_0", "cell_1", "cell_2")


def by_axis(array, axes):
    for axis in axes:
        array = lax.psum(array, axis)
    return array


def from_everyone(array, axis):
    peers = lax.axis_size(axis)
    return lax.all_to_all(
        jnp.broadcast_to(array[None], (peers, *array.shape)), axis, 0, 0, tiled=True
    )


def taken_together(array, axis):
    everything = from_everyone(array, axis)
    return jnp.sum(everything, axis=0)


def place_columns(received, positions, owned):
    local = positions[0] - lax.axis_index(CELL) * owned
    inverse = jnp.zeros((owned,), jnp.int32).at[local].set(jnp.arange(owned, dtype=jnp.int32))
    return jnp.take(received, inverse, axis=1)


def body(fractions, order, density, area, harvest):
    owned = fractions.shape[1]
    grouping = jnp.argsort(order // owned, stable=True)
    positions = jnp.take(order, grouping).reshape(1, owned)
    outgoing = jnp.take(fractions, grouping, axis=1)
    received, got_pos = (
        lax.all_to_all(outgoing, CELL, split_axis=1, concat_axis=1, tiled=True),
        lax.all_to_all(positions, CELL, split_axis=1, concat_axis=1, tiled=True),
    )
    block_frac = place_columns(received, got_pos, owned)
    matrix = block_frac.astype(jnp.float32).reshape(16, 16, owned)
    stock = area[None] * density
    total = jnp.einsum("ijc,pjc->pic", matrix, stock, precision=lax.Precision.HIGHEST)
    staying = block_frac.astype(jnp.float32)[::17]
    moved = total - staying[None] * stock
    new_stock = staying[None] * stock + (1.0 - harvest[:, None, None]) * moved
    new_area = jnp.einsum("ijc,jc->ic", matrix, area, precision=lax.Precision.HIGHEST)
    new_density = new_stock / new_area[None]
    area_cum = jnp.cumsum(new_area, axis=0) / jnp.sum(new_area, axis=0, keepdims=True)
    stock_local = jnp.sum(new_stock, axis=2)
    removed_local = jnp.sum(harvest[:, None, None] * moved, axis=(0, 2))
    stock_sums, removed_cells = (by_axis(stock_local, CELL), by_axis(removed_local, CELL))
    removed_sums = taken_together(removed_cells, "pool")
    count = lax.axis_size(CELL) * owned
    return (new_density, area_cum, stock_sums / count, removed_sums / count)


def solution(mesh):
    finer = Mesh(
        mesh.devices.reshape(8, 8, 2, mesh.shape["pool"]), ("cell_0", "cell_1", "cell_2", "pool")
    )
    return jax.shard_map(
        body,
        mesh=finer,
        in_specs=(P(None, CELL), P(CELL), P("pool", None, CELL), P(None, CELL), P("pool")),
        out_specs=(P("pool", None, CELL), P(None, CELL), P("pool", None), P()),
        check_vma=False,
    )
```

profile of v0, /device:TPU:1, one launch (start us, length us, event | category | flops | bytes accessed | tf_op | source)
XLA Modules:
  0.0 134.3 jit_solution(81761061135306279)
XLA Ops:
  0.6 0.0 copy-start.1
  0.6 0.8 add_select_fusion
  1.4 4.4 %sort.17 = (s32[1024]{0:T(1024)}, s32[1024]{0:T(1024)S(1)}) sort(s32[1024]{0:T(1024)S(1)} %add_select_fusion, s32[1024]{0:T(1024)S(1)} %iota.7), dimensions={0}, to_apply=%region_0.1 | sort | flops 10240 | bytes 16384 | tf_op jit(solution)/shard_map/jit(argsort)/sort | solution.py:36
  5.8 5.7 %gather_fusion = s32[1024]{0:T(1024)S(1)} fusion(s32[1024]{0:T(1024)} %param.8, s32[1024]{0:T(1024)S(1)} %fusion.2), kind=kCustom, calls=%fused_computation.2 | custom fusion | bytes 12288 | tf_op jit(solution)/shard_map/jit(_take)/gather | solution.py:37
  11.5 0.0 copy-start
  11.5 0.0 copy-start.2
  11.5 0.7 select_n.43
  12.2 18.4 %all-to-all-start.1 = ((s32[1,128,8]{2,0,1:T(1,128)}), s32[1,128,8]{2,0,1:T(1,128)S(1)}, u32[]{:S(2)}, u32[]{:S(2)}) async-start(s32[1,128,8]{2,0,1:T(1,128)} %bitcast.2), calls=%async_computation.1 | async-start | bytes 131072 | tf_op jit(solution)/shard_map/all_to_all | solution.py:41
  30.7 0.0 copy-done.1
  30.7 0.2 copy.77
  30.9 0.0 copy-start.3
  30.9 3.9 %gather_fusion.1 = bf16[1024,256]{1,0:T(8,128)(2,1)S(1)} fusion(bf16[256,1024]{0,1:T(8,128)(2,1)S(1)} %copy.77, s32[1024]{0:T(1024)S(1)} %fusion.2), kind=kCustom, calls=%fused_computation.clone | custom fusion | bytes 1052672 | tf_op jit(solution)/shard_map/jit(_take)/gather | solution.py:38
  34.8 1.0 select_bitcast_fusion.1
  35.8 6.2 %all-to-all-done.1 = s32[1,128,8]{2,0,1:T(1,128)S(1)} async-done(((s32[1,128,8]{2,0,1:T(1,128)}), s32[1,128,8]{2,0,1:T(1,128)S(1)}, u32[]{:S(2)}, u32[]{:S(2)}) %all-to-all-start.1) | async-done | bytes 4128 | tf_op jit(solution)/shard_map/all_to_all | solution.py:41
  42.1 7.5 %all-to-all-start = ((bf16[256,128,8]{0,2,1:T(8,128)(2,1)}), bf16[256,128,8]{0,2,1:T(8,128)(2,1)S(1)}, u32[]{:S(2)}, u32[]{:S(2)}) async-start(bf16[256,128,8]{0,2,1:T(8,128)(2,1)} %select_bitcast_fusion.1), calls=%async_computation | async-start | bytes 1048576 | tf_op jit(solution)/shard_map/all_to_all | solution.py:40
  49.6 0.0 copy-done
  49.6 0.0 copy-done.2
  49.6 0.5 copy.80
  50.2 0.0 copy-done.3
  50.2 0.2 subtract_reduce_fusion
  50.4 0.1 sub.32
  50.5 4.5 %scatter_custom_fusion = s32[1024]{0:T(1024)S(1)} fusion(s32[1024]{0:T(1024)S(1)} %bitcast.36, s32[1024]{0:T(1024)S(1)} %iota.8, s32[]{:T(128)} %constant.57.clone.1), kind=kCustom, calls=%fused_computation.29 | custom fusion | bytes 4100 | tf_op jit(solution)/shard_map/scatter | solution.py:30
  55.0 15.1 %all-to-all-done = bf16[256,128,8]{0,2,1:T(8,128)(2,1)S(1)} async-done(((bf16[256,128,8]{0,2,1:T(8,128)(2,1)}), bf16[256,128,8]{0,2,1:T(8,128)(2,1)S(1)}, u32[]{:S(2)}, u32[]{:S(2)}) %all-to-all-start) | async-done | bytes 524320 | tf_op jit(solution)/shard_map/all_to_all | solution.py:40
  70.1 3.9 %gather_fusion.2 = bf16[1024,256]{1,0:T(8,128)(2,1)S(1)} fusion(bf16[256,1024]{0,1:T(8,128)(2,1)S(1)} %bitcast.30, s32[1024]{0:T(1024)S(1)} %fusion.3), kind=kCustom, calls=%fused_computation.1.clone | custom fusion | bytes 1052672 | tf_op jit(solution)/shard_map/jit(_take)/gather | solution.py:31
  74.1 0.2 select_bitcast_fusion
  74.3 2.3 %slice.6 = bf16[16,1024]{0,1:T(8,128)(2,1)S(1)} slice(bf16[256,1024]{0,1:T(8,128)(2,1)S(1)} %select_bitcast_fusion), slice={[0:256:17], [0:1024:1]} | slice | bytes 65536 | tf_op jit(solution)/shard_map/slice | solution.py:47
  76.6 0.2 copy.79
  76.8 0.1 copy.78
  76.9 0.2 multiply_reduce_fusion
  77.2 0.1 reduce_window_sum.11
  77.2 4.7 %copy.81 = bf16[16,16,1024]{1,0,2:T(8,128)(2,1)} copy(bf16[16,16,1024]{2,1,0:T(8,128)(2,1)S(1)} %bitcast.31) | data formatting | bytes 1048576 | tf_op jit(solution)/shard_map/reshape | solution.py:44
  82.0 8.3 %fusion.7 = f32[1024,2,16]{2,1,0:T(2,128)S(1)} fusion(f32[2,16,1024]{1,0,2:T(2,128)S(1)} %copy.80, bf16[16,16,1024]{1,0,2:T(8,128)(2,1)} %copy.81), kind=kOutput, calls=%fused_computation.35 | convolution fusion | flops 6291456 | bytes 786432 | tf_op jit(solution)/shard_map/ijc,pjc->pic/dot_general | solution.py:46
  90.3 0.4 copy.82
  90.7 0.9 multiply_reduce_fusion.1
  91.6 11.9 %all-reduce.1 = (f32[2,16]{1,0:T(2,128)S(1)}, f32[16]{0:T(128)S(1)}) all-reduce(f32[2,16]{1,0:T(2,128)S(1)} %get-tuple-element.28, f32[16]{0:T(128)S(1)} %get-tuple-element.27), channel_id=1, replica_groups=mesh['cell_0'=8,'cell_1'=8,'cell_2'=2,'pool'=4] {'cell_0'}, use_global_device_ids=true, to_apply=%region_5.7 | all-reduce | flops 48 | bytes 384 | tf_op jit(solution)/shard_map/psum | solution.py:12
  103.5 11.7 %all-reduce = (f32[2,16]{1,0:T(2,128)S(1)}, f32[16]{0:T(128)S(1)}) all-reduce(f32[2,16]{1,0:T(2,128)S(1)} %get-tuple-element.31, f32[16]{0:T(128)S(1)} %get-tuple-element.32), channel_id=1, replica_groups=mesh['cell_0'=8,'cell_1'=8,'cell_2'=2,'pool'=4] {'cell_1'}, use_global_device_ids=true, to_apply=%region_6.8 | all-reduce | flops 48 | bytes 384 | tf_op jit(solution)/shard_map/psum | solution.py:12
  115.2 9.8 %all-reduce.2 = (f32[2,16]{1,0:T(2,128)S(1)}, f32[16]{0:T(128)S(1)}) all-reduce(f32[2,16]{1,0:T(2,128)S(1)} %get-tuple-element.29, f32[16]{0:T(128)S(1)} %get-tuple-element.30), channel_id=1, replica_groups=mesh['cell_0'=8,'cell_1'=8,'cell_2'=2,'pool'=4] {'cell_2'}, use_global_device_ids=true, to_apply=%region_7.9 | all-reduce | flops 48 | bytes 384 | tf_op jit(solution)/shard_map/psum | solution.py:12
  125.0 0.6 broadcast_in_dim.21
  125.6 4.0 %all-to-all-start.2 = ((f32[4,1,16]{2,1,0:T(1,128)}), f32[4,1,16]{2,1,0:T(1,128)S(1)}, u32[]{:S(2)}, u32[]{:S(2)}) async-start(f32[4,1,16]{2,1,0:T(1,128)} %broadcast_in_dim.21), calls=%async_computation.2 | async-start | bytes 4096 | tf_op jit(solution)/shard_map/all_to_all | solution.py:18
  129.6 0.6 broadcast_divide_fusion.1
  130.3 0.6 broadcast_multiply_fusion.1
  130.8 2.9 %all-to-all-done.2 = f32[4,1,16]{2,1,0:T(1,128)S(1)} async-done(((f32[4,1,16]{2,1,0:T(1,128)}), f32[4,1,16]{2,1,0:T(1,128)S(1)}, u32[]{:S(2)}, u32[]{:S(2)}) %all-to-all-start.2) | async-done | bytes 288 | tf_op jit(solution)/shard_map/all_to_all | solution.py:18
  133.8 0.5 broadcast_multiply_fusion.2
  (11 shorter events, 0.1 us)
Async XLA Ops:
  0.6 30.0 %copy-start.1 = (bf16[256,1024]{1,0:T(8,128)(2,1)S(1)}, bf16[256,1024]{1,0:T(8,128)(2,1)}, u32[]{:S(2)}) copy-start(bf16[256,1024]{1,0:T(8,128)(2,1)} %param.7) | copy-start | bytes 1572868
  11.5 38.1 %copy-start = (f32[16,1024]{1,0:T(8,128)S(1)}, f32[16,1024]{1,0:T(8,128)}, u32[]{:S(2)}) copy-start(f32[16,1024]{1,0:T(8,128)} %param.10) | copy-start | bytes 196612
  11.5 38.1 %copy-start.2 = (f32[2,16,1024]{2,1,0:T(8,128)S(1)}, f32[2,16,1024]{2,1,0:T(8,128)}, u32[]{:S(2)}) copy-start(f32[2,16,1024]{2,1,0:T(8,128)} %param.9) | copy-start | bytes 393220
  12.2 29.8 %all-to-all-start.1 = ((s32[1,128,8]{2,0,1:T(1,128)}), s32[1,128,8]{2,0,1:T(1,128)S(1)}, u32[]{:S(2)}, u32[]{:S(2)}) async-start(s32[1,128,8]{2,0,1:T(1,128)} %bitcast.2), calls=%async_computation.1 | async-start | bytes 131072 | tf_op jit(solution)/shard_map/all_to_all | solution.py:41
  30.9 19.3 %copy-start.3 = (f32[2]{0:T(128)S(1)}, f32[2]{0:T(128)}, u32[]{:S(2)}) copy-start(f32[2]{0:T(128)} %param.11) | copy-start | bytes 28
  42.1 28.1 %all-to-all-start = ((bf16[256,128,8]{0,2,1:T(8,128)(2,1)}), bf16[256,128,8]{0,2,1:T(8,128)(2,1)S(1)}, u32[]{:S(2)}, u32[]{:S(2)}) async-start(bf16[256,128,8]{0,2,1:T(8,128)(2,1)} %select_bitcast_fusion.1), calls=%async_computation | async-start | bytes 1048576 | tf_op jit(solution)/shard_map/all_to_all | solution.py:40
  125.6 8.1 %all-to-all-start.2 = ((f32[4,1,16]{2,1,0:T(1,128)}), f32[4,1,16]{2,1,0:T(1,128)S(1)}, u32[]{:S(2)}, u32[]{:S(2)}) async-start(f32[4,1,16]{2,1,0:T(1,128)} %broadcast_in_dim.21), calls=%async_computation.2 | async-start | bytes 4096 | tf_op jit(solution)/shard_map/all_to_all | solution.py:18
where the time goes:
time: 135 us; the launch traced here: 134 us
  blocking collectives  33.4 us (25%)
  starting transfers between devices  29.9 us (22%)
  local copies, waits for them, and re-layouts  28 us (21%)
  waiting for transfers between devices  24.3 us (18%)
  other arithmetic  9.47 us (7%)
  matrix products  8.33 us (6%)
    psum x3, blocking collectives, by_axis(): array = lax.psum(array, axis)  33.4 us
    all_to_all x1, starting transfers between devices, body(): lax.all_to_all(positions, CELL, split_axis=1, concat_axis=1, tiled=True)  18.4 us
    all_to_all x1, waiting for transfers between devices, body(): lax.all_to_all(outgoing, CELL, split_axis=1, concat_axis=1, tiled=True)  15.1 us
    dot_general x1, matrix products, body(): jnp.einsum('ijc,pjc->pic', matrix, stock, precision=lax.Precision.HIGHEST)  8.33 us
    all_to_all x1, starting transfers between devices, body(): lax.all_to_all(outgoing, CELL, split_axis=1, concat_axis=1, tiled=True)  7.49 us
    all_to_all x1, waiting for transfers between devices, body(): lax.all_to_all(positions, CELL, split_axis=1, concat_axis=1, tiled=True)  6.24 us
    gather x1, local copies, waits for them, and re-layouts, body(): positions = jnp.take(order, grouping).reshape(1, owned)  5.72 us
    reshape x1, local copies, waits for them, and re-layouts, body(): matrix = block_frac.astype(jnp.float32).reshape(16, 16, owned)  4.73 us
  transfers between devices with their start and end apart: 3, of which 3 were waited for; matrix products, arithmetic and copies ran while one was open for 9% of the time, Pallas kernels for 0%

commit v1 on v0

v1 whole, which is shorter than its diff:
```python
import functools

import jax
import jax.numpy as jnp
from jax import lax
from jax.experimental import pallas as pl
from jax.experimental.pallas import tpu as pltpu
from jax.sharding import Mesh
from jax.sharding import PartitionSpec as P

MESH = pl.DeviceIdType.MESH
F32, BF16, I32 = jnp.float32, jnp.bfloat16, jnp.int32
TYPES = 16


def nt(a, b):
    return lax.dot_general(a, b, (((1,), (1,)), ((), ())), preferred_element_type=F32)


def iota(shape, dim):
    return lax.broadcasted_iota(I32, shape, dim)


def kernel(dims, frac, order, dens, area, harv, out_dens, out_cum, out_mean, out_rem,
           f2, ordv, areav, hsm, hs, hg, dg, stock, oh, psend, pa, ps2, pb, sd, av, bv,
           mv, snd, snd_a, rcv, rcv_a, red0, red1, red2, red3, red4, red5, lsem,
           d_s, d_r, h_s, h_r, p1_s, p1_r, s1_s, s1_r, p2_s, p2_r, s2_s, s2_r,
           o_s, o_r, a_s, a_r, r1_s, r1_r, r2_s, r2_r, r3_s, r3_r):
    nz, ny, nc, nx, cells = dims
    ns = nz * nc
    rank_n = 128 // ns
    half_n = rank_n // 2
    owned = 128 * ny
    rows = 256 // nx
    il_n = TYPES // nx
    pools = 2 * nx
    z, y, c, x = (lax.axis_index(a) for a in ("z", "y", "core", "pool"))
    me = z * nc + c

    def dev_s(o):
        t = lax.rem(me + o, ns)
        return t, (t // nc, y, lax.rem(t, nc), x)

    def dev_y(o):
        t = lax.rem(y + o, ny)
        return t, (z, t, c, x)

    def dev_x(o):
        t = lax.rem(x + o, nx)
        return t, (z, y, c, t)

    local = [
        pltpu.make_async_copy(order, ordv, lsem.at[0]),
        pltpu.make_async_copy(frac.at[pl.ds(pl.multiple_of(x * rows, rows), rows), :], f2.at[pl.ds(0, rows), :], lsem.at[1]),
        pltpu.make_async_copy(frac.at[pl.ds(pl.multiple_of(x * rows, rows), rows), :], f2.at[pl.ds(rows, rows), :], lsem.at[2]),
        pltpu.make_async_copy(area, areav, lsem.at[3]),
        pltpu.make_async_copy(dens, dg.at[pl.ds(2 * x, 2)], lsem.at[4]),
    ]
    for cp in local:
        cp.start()

    barrier = pltpu.get_barrier_semaphore()
    peers = [dev_x(o)[1] for o in range(1, nx)]
    peers += [dev_y(o)[1] for o in range(1, ny)]
    peers += [dev_s(o)[1] for o in range(1, ns)]
    for p in peers:
        pl.semaphore_signal(barrier, inc=1, device_id=p, device_id_type=MESH)

    row8 = iota((8, 128), 0)
    lane8 = iota((8, 128), 1)
    hval = jnp.where(row8 == 2 * x, harv[0], jnp.where(row8 == 2 * x + 1, harv[1], 0.0))
    hs[...] = hval

    local[0].wait()
    ordr = ordv[...]
    dest = ordr // owned
    pos = lax.rem(ordr, owned)
    dz, dy, dc = dest // (ny * nc), lax.rem(dest // nc, ny), lax.rem(dest, nc)
    group = (dz * nc + dc) * ny + dy
    groups = ns * ny
    upper = (iota((128, 128), 0) < iota((128, 128), 1)).astype(BF16)
    ones = jnp.ones((128, 128), BF16)
    before = jnp.zeros((groups, 128), F32)
    ranks = []
    for b in range(ny):
        hot = iota((groups, 128), 0) == group[b:b + 1, :]
        hotb = hot.astype(BF16)
        oh[:, b * 128:(b + 1) * 128] = hotb
        count = jnp.dot(hotb, upper, preferred_element_type=F32) + before
        if b < ny - 1:
            before = before + jnp.dot(hotb, ones, preferred_element_type=F32)
        ranks.append(jnp.sum(jnp.where(hot, count, 0.0), axis=0, keepdims=True))
    rank = jnp.concatenate(ranks, axis=0).astype(I32)
    part = rank // half_n
    sub = lax.rem(rank, half_n)

    lane_of = part * (ns * half_n) + me * half_n + sub
    hi = (pos // 32).astype(F32)
    lo = lax.rem(pos, 32).astype(F32)
    acc_hi = jnp.zeros((groups, 128), F32)
    acc_lo = jnp.zeros((groups, 128), F32)
    for b in range(ny):
        hot = oh[:, b * 128:(b + 1) * 128]
        sel = iota((128, 128), 0) == lane_of[b:b + 1, :]
        acc_hi += nt(hot, jnp.where(sel, hi[b:b + 1, :], 0.0).astype(BF16))
        acc_lo += nt(hot, jnp.where(sel, lo[b:b + 1, :], 0.0).astype(BF16))
    psend[...] = (acc_hi * 32.0 + acc_lo).reshape(ns, ny, 128)

    pl.semaphore_wait(barrier, len(peers))

    sends = []

    def send(src, dst, ss, rs, to):
        cp = pltpu.make_async_remote_copy(src_ref=src, dst_ref=dst, send_sem=ss, recv_sem=rs,
                                          device_id=to, device_id_type=MESH)
        cp.start()
        sends.append(cp)
        return cp

    far_s = sorted(range(1, ns), key=lambda o: -min(o, ns - o))
    far_y = sorted(range(1, ny), key=lambda o: -min(o, ny - o))
    far_x = sorted(range(1, nx), key=lambda o: -min(o, nx - o))

    p1 = []
    for o in far_s:
        t, to = dev_s(o)
        p1.append(send(psend.at[t], pa.at[me], p1_s.at[o], p1_r.at[o], to))

    key = group * half_n + sub
    rho = groups * half_n
    local[1].wait()
    local[2].wait()
    halves = []
    for h in range(2):
        keyh = jnp.where(part == h, key, -1)
        hots = [(iota((rho, 128), 0) == keyh[b:b + 1, :]).astype(BF16) for b in range(ny)]
        halves.append(nt(jnp.concatenate(hots, axis=1), f2[...]))
    lanes = iota((rho, 128), 1)
    moved_cols = jnp.where(lanes < rows, halves[0], halves[1]).astype(BF16)
    sd[...] = moved_cols.reshape(ns, ny, half_n, 128)

    s1 = []
    for o in far_s:
        t, to = dev_s(o)
        s1.append(send(sd.at[t], av.at[me], s1_s.at[o], s1_r.at[o], to))
    av[pl.ds(me, 1)] = sd[pl.ds(me, 1)]
    pa[pl.ds(me, 1)] = psend[pl.ds(me, 1)]

    dcp, hcp = [], []
    for o in far_x:
        t, to = dev_x(o)
        hcp.append(send(hs, hg.at[x], h_s.at[o], h_r.at[o], to))
        dcp.append(send(dens, dg.at[pl.ds(2 * x, 2)], d_s.at[o], d_r.at[o], to))
    hg[pl.ds(x, 1)] = hs[...].reshape(1, 8, 128)

    for cp in p1:
        cp.wait_recv()
    ptot = pa[0]
    for s in range(1, ns):
        ptot = ptot + pa[s]
    ps2[...] = ptot.reshape(ny, 1, 128)
    p2 = []
    for o in far_y:
        t, to = dev_y(o)
        p2.append(send(ps2.at[t], pb.at[y], p2_s.at[o], p2_r.at[o], to))
    pb[pl.ds(y, 1)] = ps2[pl.ds(y, 1)]

    for cp in s1:
        cp.wait_recv()
    s2 = []
    for o in far_y:
        t, to = dev_y(o)
        s2.append(send(av.at[:, t], bv.at[y], s2_s.at[o], s2_r.at[o], to))
    bv[pl.ds(y, 1)] = av[:, pl.ds(y, 1)].reshape(1, ns, half_n, 128)

    for cp in hcp:
        cp.wait_recv()
    harvest = hg[0]
    for s in range(1, nx):
        harvest = harvest + hg[s]
    local[3].wait()
    local[4].wait()
    for cp in dcp:
        cp.wait_recv()
    for j in range(TYPES):
        stock[j] = dg[:, j, :] * areav[j:j + 1, :]

    for cp in p2:
        cp.wait_recv()
    low = iota((1, 128), 1) < 64
    hots = [[], []]
    for q in range(ny // 2):
        a, b = pb[2 * q], pb[2 * q + 1]
        ra, rb = pltpu.roll(a, 64, 1), pltpu.roll(b, 64, 1)
        for h, v in enumerate((jnp.where(low, a, rb), jnp.where(low, ra, b))):
            hots[h].append((iota((owned, 128), 0) == v.astype(I32)).astype(BF16))
    spread = [jnp.concatenate(v, axis=1) for v in hots]

    for cp in s2:
        cp.wait_recv()
    turned = bv[...].reshape(ny * ns * half_n, 128).T
    mv[...] = nt(turned[:rows], spread[0]) + nt(turned[rows:], spread[1])

    keep = 1.0 - harvest
    zero = jnp.zeros((8, 128), F32)

    def block(lb, carry):
        sums, gone = carry
        cols = pl.ds(pl.multiple_of(lb * 128, 128), 128)
        new_sums, new_gone = [], []
        for il in range(il_n):
            tot, na, stay = zero, zero, zero
            for j in range(TYPES):
                m = jnp.broadcast_to(mv[il * TYPES + j:il * TYPES + j + 1, cols], (8, 128))
                term = m * stock[j, :, cols]
                tot = tot + term
                if j % il_n == il:
                    stay = jnp.where(x == j // il_n, term, stay)
                na = na + m * jnp.broadcast_to(areav[j:j + 1, cols], (8, 128))
            moved = tot - stay
            ns_i = stay + keep * moved
            new_sums.append(sums[il] + ns_i)
            new_gone.append(gone[il] + harvest * moved)
            snd[:, il, cols] = ns_i / na
            snd_a[il:il + 1, cols] = na[0:1]
        return tuple(new_sums), tuple(new_gone)

    zeros = (zero,) * il_n
    sums, gone = lax.fori_loop(0, ny, block, (zeros, zeros))

    ocp = []
    for o in far_x:
        t, to = dev_x(o)
        ocp.append(send(snd_a, rcv_a.at[x], a_s.at[o], a_r.at[o], to))
        ocp.append(send(snd.at[pl.ds(2 * t, 2)], rcv.at[x], o_s.at[o], o_r.at[o], to))

    word = zero
    for il in range(il_n):
        i = il_n * x + il
        word = jnp.where(lane8 == i, jnp.sum(sums[il], axis=1, keepdims=True), word)
        word = jnp.where(lane8 == TYPES + i, jnp.sum(gone[il], axis=1, keepdims=True), word)
    red0[...] = word
    rc = []
    for o in far_s:
        t, to = dev_s(o)
        rc.append(send(red0, red1.at[me], r1_s.at[o], r1_r.at[o], to))
    red1[pl.ds(me, 1)] = word.reshape(1, 8, 128)
    rcv[pl.ds(x, 1)] = snd[pl.ds(2 * x, 2)].reshape(1, 2, il_n, owned)
    rcv_a[pl.ds(x, 1)] = snd_a[...].reshape(1, il_n, owned)
    for cp in rc:
        cp.wait_recv()
    tot = red1[0]
    for s in range(1, ns):
        tot = tot + red1[s]
    red2[...] = tot
    rc = []
    for o in far_y:
        t, to = dev_y(o)
        rc.append(send(red2, red3.at[y], r2_s.at[o], r2_r.at[o], to))
    red3[pl.ds(y, 1)] = tot.reshape(1, 8, 128)

    for cp in ocp:
        cp.wait_recv()
    run = None
    for i in range(TYPES):
        xs, il = i // il_n, i % il_n
        r = rcv_a[xs, il:il + 1, :]
        run = r if run is None else run + r
        out_cum[i:i + 1, :] = run
        for q in range(2):
            out_dens[q, i:i + 1, :] = rcv[xs, q, il:il + 1, :]
    out_cum[...] = out_cum[...] / run

    for cp in rc:
        cp.wait_recv()
    tot = red3[0]
    for s in range(1, ny):
        tot = tot + red3[s]
    red4[...] = tot
    rc = []
    for o in far_x:
        t, to = dev_x(o)
        rc.append(send(red4, red5.at[x], r3_s.at[o], r3_r.at[o], to))
    red5[pl.ds(x, 1)] = tot.reshape(1, 8, 128)
    for cp in rc:
        cp.wait_recv()
    tot = red5[0]
    for s in range(1, nx):
        tot = tot + red5[s]
    tot = tot / cells
    red4_out = tot
    red0_out = jnp.sum(pltpu.roll(tot, 128 - TYPES, 1), axis=0, keepdims=True)
    out_rem[...] = red0_out[:, :TYPES]
    hs_pick = jnp.zeros((2, 128), F32)
    for q in range(2):
        pick = jnp.sum(jnp.where(row8 == 2 * x + q, red4_out, 0.0), axis=0, keepdims=True)
        hs_pick = jnp.where(iota((2, 128), 0) == q, pick, hs_pick)
    out_mean[...] = hs_pick[:, :TYPES]
    for cp in sends:
        cp.wait_send()


def solution(mesh):
    nx = mesh.shape["pool"]
    nc = 2
    ncell = mesh.shape["cell"]
    nz = ny = int(round((ncell // nc) ** 0.5))
    finer = Mesh(mesh.devices.reshape(nz, ny, nc, nx), ("z", "y", "core", "pool"))
    ns = nz * nc
    half_n = 64 // ns
    owned = 128 * ny
    rows = 256 // nx
    il_n = TYPES // nx
    groups = ns * ny
    dims = (nz, ny, nc, nx, float(ncell * owned))
    any_, vm = pl.BlockSpec(memory_space=pl.ANY), pl.BlockSpec(memory_space=pltpu.VMEM)
    sm = pl.BlockSpec(memory_space=pltpu.SMEM)
    dma = pltpu.SemaphoreType.DMA

    def body(fractions, order, density, area, harvest):
        scratch = [
            pltpu.VMEM((2 * rows, owned), BF16),
            pltpu.VMEM((ny, 128), I32),
            pltpu.VMEM((TYPES, owned), F32),
            pltpu.SMEM((2,), F32),
            pltpu.VMEM((8, 128), F32),
            pltpu.VMEM((nx, 8, 128), F32),
            pltpu.VMEM((2 * nx, TYPES, owned), F32),
            pltpu.VMEM((TYPES, 2 * nx, owned), F32),
            pltpu.VMEM((groups, owned), BF16),
            pltpu.VMEM((ns, ny, 128), F32),
            pltpu.VMEM((ns, ny, 128), F32),
            pltpu.VMEM((ny, 1, 128), F32),
            pltpu.VMEM((ny, 1, 128), F32),
            pltpu.VMEM((ns, ny, half_n, 128), BF16),
            pltpu.VMEM((ns, ny, half_n, 128), BF16),
            pltpu.VMEM((ny, ns, half_n, 128), BF16),
            pltpu.VMEM((rows, owned), F32),
            pltpu.VMEM((2 * nx, il_n, owned), F32),
            pltpu.VMEM((il_n, owned), F32),
            pltpu.VMEM((nx, 2, il_n, owned), F32),
            pltpu.VMEM((nx, il_n, owned), F32),
            pltpu.VMEM((8, 128), F32),
            pltpu.VMEM((ns, 8, 128), F32),
            pltpu.VMEM((8, 128), F32),
            pltpu.VMEM((ny, 8, 128), F32),
            pltpu.VMEM((8, 128), F32),
            pltpu.VMEM((nx, 8, 128), F32),
            dma((5,)),
        ]
        for n in (nx, nx, ns, ns, ny, ny, nx, nx, ns, ny, nx):
            scratch += [dma((n,)), dma((n,))]
        dens, cum, mean, rem = pl.pallas_call(
            functools.partial(kernel, dims),
            out_shape=(
                jax.ShapeDtypeStruct((2, TYPES, owned), F32),
                jax.ShapeDtypeStruct((TYPES, owned), F32),
                jax.ShapeDtypeStruct((2, TYPES), F32),
                jax.ShapeDtypeStruct((1, TYPES), F32),
            ),
            in_specs=[any_, any_, any_, any_, sm],
            out_specs=(vm, vm, vm, vm),
            scratch_shapes=scratch,
            compiler_params=pltpu.CompilerParams(collective_id=0, has_side_effects=True),
        )(fractions, order.reshape(ny, 128), density, area, harvest)
        return dens, cum, mean, rem.reshape(TYPES)

    cell = ("z", "y", "core")
    return jax.shard_map(
        body,
        mesh=finer,
        in_specs=(P(None, cell), P(cell), P("pool", None, cell), P(None, cell), P("pool")),
        out_specs=(P("pool", None, cell), P(None, cell), P("pool", None), P()),
        check_vma=False,
    )
```

time: 135 us -> 47.7 us (0.35)
  Pallas kernels: 0 us -> 43.4 us
  blocking collectives: 33.4 us -> 0 us
  starting transfers between devices: 29.9 us -> 0 us
  local copies, waits for them, and re-layouts: 28 us -> 3.4 us
  waiting for transfers between devices: 24.3 us -> 0 us
  other arithmetic: 9.47 us -> 0 us
  matrix products: 8.33 us -> 0 us
    pallas_call x0 -> x1, Pallas kernels: none -> 43.4 us  [body(): pl.pallas_call(functools.partial(kernel, dims), out_shape=(jax.ShapeDtype...]
    psum x3 -> x0, blocking collectives: 33.4 us -> none  [by_axis(): array = lax.psum(array, axis)]
    all_to_all x3 -> x0, starting transfers between devices: 29.9 us -> none  [the longest x1 18.4 us: body(): lax.all_to_all(positions, CELL, split_axis=1, concat_axis=1, tiled=True)]
    all_to_all x3 -> x0, waiting for transfers between devices: 24.3 us -> none  [the longest x1 15.1 us: body(): lax.all_to_all(outgoing, CELL, split_axis=1, concat_axis=1, tiled=True)]
    gather x3 -> x0, local copies, waits for them, and re-layouts: 13.6 us -> none  [the longest x1 5.72 us: body(): positions = jnp.take(order, grouping).reshape(1, owned)]
    dot_general x1 -> x0, matrix products: 8.33 us -> none  [body(): jnp.einsum('ijc,pjc->pic', matrix, stock, precision=lax.Precision.HIGHEST)]
    reshape x1 -> x0, local copies, waits for them, and re-layouts: 4.73 us -> none  [body(): matrix = block_frac.astype(jnp.float32).reshape(16, 16, owned)]
    scatter x1 -> x0, local copies, waits for them, and re-layouts: 4.49 us -> none  [place_columns(): jnp.zeros((owned,), jnp.int32).at[local]]
  transfers between devices with their start and end apart: 3 -> 0, of which waited for: 3 -> 0; matrix products, arithmetic and copies ran while one was open for 9% -> 0% of each run, Pallas kernels for 0% -> 0%
where the time goes in v1:
time: 47.7 us; the launch traced here: 47.5 us
  Pallas kernels  43.4 us (91%)
  local copies, waits for them, and re-layouts  3.4 us (7%)
  between operations  0.65 us (1%)
    pallas_call x1, Pallas kernels, body(): pl.pallas_call(functools.partial(kernel, dims), out_shape=(jax.ShapeDtype...  43.4 us
    unnamed x10, local copies, waits for them, and re-layouts  3.4 us

profile of v1, /device:TPU:1, one launch (start us, length us, event | category | flops | bytes accessed | tf_op | source)
XLA Modules:
  0.0 47.5 jit_solution(7547151715950086058)
XLA Ops:
  0.6 43.4 %shard_map.84 = (f32[2,16,1024]{2,1,0:T(8,128)}, f32[16,1024]{1,0:T(8,128)}, f32[2,16]{1,0:T(2,128)}, f32[1,16]{1,0:T(1,128)}) custom-call(bf16[256,1024]{1,0:T(8,128)(2,1)} %frac.1, s32[8,128]{1,0:T(8,128)} %bitcast.2, f32[2,16,1024]{2,1,0:T(8,128)} %dens.1, f32[16,1024]{1,0:T(8,128)} %area.1, f32[2]{0:T(128)} %harv.1), custom_call_target="tpu_custom_call" | custom-call | tf_op jit(solution)/shard_map/pallas_call | solution.py:353
  44.1 0.0 copy-start
  44.1 1.6 %copy.13 = f32[2,16,1024]{2,1,0:T(8,128)} copy(f32[2,16,1024]{2,1,0:T(8,128)} %get-tuple-element.16) | data formatting | bytes 262144
  45.7 0.0 copy-done
  45.7 0.0 copy-start.1
  45.7 0.6 %copy.14 = f32[16,1024]{1,0:T(8,128)} copy(f32[16,1024]{1,0:T(8,128)S(1)} %copy-done) | data formatting | bytes 131072
  46.3 0.0 copy-done.1
  46.3 0.0 copy-start.2
  46.3 0.6 %copy.15 = f32[2,16]{1,0:T(2,128)} copy(f32[2,16]{1,0:T(2,128)S(1)} %copy-done.1) | data formatting | bytes 256
  46.9 0.1 copy-done.2
  47.0 0.5 %copy.16 = f32[16]{0:T(128)} copy(f32[16]{0:T(128)S(1)} %bitcast.3) | data formatting | bytes 128
Async XLA Ops:
  44.1 1.6 %copy-start = (f32[16,1024]{1,0:T(8,128)S(1)}, f32[16,1024]{1,0:T(8,128)}, u32[]{:S(2)}) copy-start(f32[16,1024]{1,0:T(8,128)} %get-tuple-element.17) | copy-start | bytes 196612
  45.7 0.7 %copy-start.1 = (f32[2,16]{1,0:T(2,128)S(1)}, f32[2,16]{1,0:T(2,128)}, u32[]{:S(2)}) copy-start(f32[2,16]{1,0:T(2,128)} %get-tuple-element.18) | copy-start | bytes 388
  46.3 0.6 %copy-start.2 = (f32[1,16]{1,0:T(1,128)S(1)}, f32[1,16]{1,0:T(1,128)}, u32[]{:S(2)}) copy-start(f32[1,16]{1,0:T(1,128)} %get-tuple-element.11) | copy-start | bytes 196

commit v2 on v1

--- a/solution.py
+++ b/solution.py
@@ -11,6 +11,7 @@
 MESH = pl.DeviceIdType.MESH
 F32, BF16, I32 = jnp.float32, jnp.bfloat16, jnp.int32
 TYPES = 16
+VMEM_LIMIT = 12 * 1024 * 1024
 
 
 def nt(a, b):
@@ -21,11 +22,20 @@
     return lax.broadcasted_iota(I32, shape, dim)
 
 
+def hand_over(*refs):
+    sem = refs[8]
+    copies = [pltpu.make_async_copy(refs[i], refs[4 + i], sem.at[i]) for i in range(4)]
+    for cp in copies:
+        cp.start()
+    for cp in copies:
+        cp.wait()
+
+
 def kernel(dims, frac, order, dens, area, harv, out_dens, out_cum, out_mean, out_rem,
            f2, ordv, areav, hsm, hs, hg, dg, stock, oh, psend, pa, ps2, pb, sd, av, bv,
-           mv, snd, snd_a, rcv, rcv_a, red0, red1, red2, red3, red4, red5, lsem,
+           mv, snd, snd_a, rcv, rcv_a, red0, red1, red2, red3, lsem,
            d_s, d_r, h_s, h_r, p1_s, p1_r, s1_s, s1_r, p2_s, p2_r, s2_s, s2_r,
-           o_s, o_r, a_s, a_r, r1_s, r1_r, r2_s, r2_r, r3_s, r3_r):
+           o_s, o_r, a_s, a_r, r1_s, r1_r, r2_s, r2_r):
     nz, ny, nc, nx, cells = dims
     ns = nz * nc
     rank_n = 128 // ns
@@ -49,27 +59,25 @@
         t = lax.rem(x + o, nx)
         return t, (z, y, c, t)
 
+    def dev_yx(o):
+        return z, lax.rem(y + o // nx, ny), c, lax.rem(x + o % nx, nx)
+
     local = [
         pltpu.make_async_copy(order, ordv, lsem.at[0]),
         pltpu.make_async_copy(frac.at[pl.ds(pl.multiple_of(x * rows, rows), rows), :], f2.at[pl.ds(0, rows), :], lsem.at[1]),
         pltpu.make_async_copy(frac.at[pl.ds(pl.multiple_of(x * rows, rows), rows), :], f2.at[pl.ds(rows, rows), :], lsem.at[2]),
         pltpu.make_async_copy(area, areav, lsem.at[3]),
         pltpu.make_async_copy(dens, dg.at[pl.ds(2 * x, 2)], lsem.at[4]),
+        pltpu.make_async_copy(harv, hsm, lsem.at[5]),
     ]
     for cp in local:
         cp.start()
 
     barrier = pltpu.get_barrier_semaphore()
-    peers = [dev_x(o)[1] for o in range(1, nx)]
-    peers += [dev_y(o)[1] for o in range(1, ny)]
+    peers = [dev_yx(o) for o in range(1, ny * nx)]
     peers += [dev_s(o)[1] for o in range(1, ns)]
     for p in peers:
         pl.semaphore_signal(barrier, inc=1, device_id=p, device_id_type=MESH)
-
-    row8 = iota((8, 128), 0)
-    lane8 = iota((8, 128), 1)
-    hval = jnp.where(row8 == 2 * x, harv[0], jnp.where(row8 == 2 * x + 1, harv[1], 0.0))
-    hs[...] = hval
 
     local[0].wait()
     ordr = ordv[...]
@@ -106,8 +114,6 @@
         acc_lo += nt(hot, jnp.where(sel, lo[b:b + 1, :], 0.0).astype(BF16))
     psend[...] = (acc_hi * 32.0 + acc_lo).reshape(ns, ny, 128)
 
-    pl.semaphore_wait(barrier, len(peers))
-
     sends = []
 
     def send(src, dst, ss, rs, to):
@@ -119,12 +125,9 @@
 
     far_s = sorted(range(1, ns), key=lambda o: -min(o, ns - o))
     far_y = sorted(range(1, ny), key=lambda o: -min(o, ny - o))
+    far_yx = sorted(range(1, ny * nx), key=lambda o: -min(o // nx, ny - o // nx) - min(o % nx, nx - o % nx))
+    slot = {o: ny - 1 - far_y.index(o) for o in far_y}
     far_x = sorted(range(1, nx), key=lambda o: -min(o, nx - o))
-
-    p1 = []
-    for o in far_s:
-        t, to = dev_s(o)
-        p1.append(send(psend.at[t], pa.at[me], p1_s.at[o], p1_r.at[o], to))
 
     key = group * half_n + sub
     rho = groups * half_n
@@ -139,18 +142,23 @@
     moved_cols = jnp.where(lanes < rows, halves[0], halves[1]).astype(BF16)
     sd[...] = moved_cols.reshape(ns, ny, half_n, 128)
 
-    s1 = []
+    local[5].wait()
+    row8, lane8 = iota((8, 128), 0), iota((8, 128), 1)
+    hs[...] = jnp.where(row8 == 2 * x, hsm[0], jnp.where(row8 == 2 * x + 1, hsm[1], 0.0))
+
+    pl.semaphore_wait(barrier, len(peers))
+    p1, s1 = [], []
     for o in far_s:
         t, to = dev_s(o)
+        p1.append(send(psend.at[t], pa.at[me], p1_s.at[o], p1_r.at[o], to))
         s1.append(send(sd.at[t], av.at[me], s1_s.at[o], s1_r.at[o], to))
-    av[pl.ds(me, 1)] = sd[pl.ds(me, 1)]
-    pa[pl.ds(me, 1)] = psend[pl.ds(me, 1)]
-
     dcp, hcp = [], []
     for o in far_x:
         t, to = dev_x(o)
         hcp.append(send(hs, hg.at[x], h_s.at[o], h_r.at[o], to))
         dcp.append(send(dens, dg.at[pl.ds(2 * x, 2)], d_s.at[o], d_r.at[o], to))
+    av[pl.ds(me, 1)] = sd[pl.ds(me, 1)]
+    pa[pl.ds(me, 1)] = psend[pl.ds(me, 1)]
     hg[pl.ds(x, 1)] = hs[...].reshape(1, 8, 128)
 
     for cp in p1:
@@ -162,16 +170,16 @@
     p2 = []
     for o in far_y:
         t, to = dev_y(o)
-        p2.append(send(ps2.at[t], pb.at[y], p2_s.at[o], p2_r.at[o], to))
-    pb[pl.ds(y, 1)] = ps2[pl.ds(y, 1)]
+        p2.append(send(ps2.at[t], pb.at[slot[o]], p2_s.at[o], p2_r.at[o], to))
+    pb[0:1] = ps2[pl.ds(y, 1)]
 
     for cp in s1:
         cp.wait_recv()
     s2 = []
     for o in far_y:
         t, to = dev_y(o)
-        s2.append(send(av.at[:, t], bv.at[y], s2_s.at[o], s2_r.at[o], to))
-    bv[pl.ds(y, 1)] = av[:, pl.ds(y, 1)].reshape(1, ns, half_n, 128)
+        s2.append(send(av.at[:, t], bv.at[slot[o]], s2_s.at[o], s2_r.at[o], to))
+    bv[0:1] = av[:, pl.ds(y, 1)].reshape(1, ns, half_n, 128)
 
     for cp in hcp:
         cp.wait_recv()
@@ -196,10 +204,17 @@
             hots[h].append((iota((owned, 128), 0) == v.astype(I32)).astype(BF16))
     spread = [jnp.concatenate(v, axis=1) for v in hots]
 
-    for cp in s2:
-        cp.wait_recv()
-    turned = bv[...].reshape(ny * ns * half_n, 128).T
-    mv[...] = nt(turned[:rows], spread[0]) + nt(turned[rows:], spread[1])
+    per = ny // 2
+    width = per * ns * half_n
+    for g in range(2):
+        for o, cp in zip(far_y, s2):
+            if slot[o] // per == g:
+                cp.wait_recv()
+        turned = bv[g * per:(g + 1) * per].reshape(width, 128).T
+        got = [nt(turned[h * rows:(h + 1) * rows], spread[h][:, g * width:(g + 1) * width]) for h in range(2)]
+        if g == 0:
+            near = got[0] + got[1]
+    mv[...] = near + (got[0] + got[1])
 
     keep = 1.0 - harvest
     zero = jnp.zeros((8, 128), F32)
@@ -236,15 +251,15 @@
 
     word = zero
     for il in range(il_n):
-        i = il_n * x + il
-        word = jnp.where(lane8 == i, jnp.sum(sums[il], axis=1, keepdims=True), word)
-        word = jnp.where(lane8 == TYPES + i, jnp.sum(gone[il], axis=1, keepdims=True), word)
+        word = jnp.where(lane8 == row8 * il_n + il, jnp.sum(sums[il], axis=1, keepdims=True), word)
+        word = jnp.where(lane8 == 8 * il_n + il, jnp.sum(gone[il], axis=1, keepdims=True), word)
+    word = jnp.sum(word, axis=0, keepdims=True)
     red0[...] = word
     rc = []
     for o in far_s:
         t, to = dev_s(o)
         rc.append(send(red0, red1.at[me], r1_s.at[o], r1_r.at[o], to))
-    red1[pl.ds(me, 1)] = word.reshape(1, 8, 128)
+    red1[pl.ds(me, 1)] = word.reshape(1, 1, 128)
     rcv[pl.ds(x, 1)] = snd[pl.ds(2 * x, 2)].reshape(1, 2, il_n, owned)
     rcv_a[pl.ds(x, 1)] = snd_a[...].reshape(1, il_n, owned)
     for cp in rc:
@@ -254,10 +269,10 @@
         tot = tot + red1[s]
     red2[...] = tot
     rc = []
-    for o in far_y:
-        t, to = dev_y(o)
-        rc.append(send(red2, red3.at[y], r2_s.at[o], r2_r.at[o], to))
-    red3[pl.ds(y, 1)] = tot.reshape(1, 8, 128)
+    for o in far_yx:
+        to = dev_yx(o)
+        rc.append(send(red2, red3.at[y * nx + x], r2_s.at[o], r2_r.at[o], to))
+    red3[pl.ds(y * nx + x, 1)] = tot.reshape(1, 1, 128)
 
     for cp in ocp:
         cp.wait_recv()
@@ -273,29 +288,22 @@
 
     for cp in rc:
         cp.wait_recv()
-    tot = red3[0]
-    for s in range(1, ny):
-        tot = tot + red3[s]
-    red4[...] = tot
-    rc = []
-    for o in far_x:
-        t, to = dev_x(o)
-        rc.append(send(red4, red5.at[x], r3_s.at[o], r3_r.at[o], to))
-    red5[pl.ds(x, 1)] = tot.reshape(1, 8, 128)
-    for cp in rc:
-        cp.wait_recv()
-    tot = red5[0]
-    for s in range(1, nx):
-        tot = tot + red5[s]
-    tot = tot / cells
-    red4_out = tot
-    red0_out = jnp.sum(pltpu.roll(tot, 128 - TYPES, 1), axis=0, keepdims=True)
-    out_rem[...] = red0_out[:, :TYPES]
-    hs_pick = jnp.zeros((2, 128), F32)
+    lane1 = iota((1, 128), 1)
+    mean = [jnp.zeros((1, 128), F32)] * 2
+    rem = jnp.zeros((1, 128), F32)
+    for xs in range(nx):
+        tot = red3[xs]
+        for s in range(1, ny):
+            tot = tot + red3[s * nx + xs]
+        tot = tot / cells
+        here = lane1 // il_n == xs
+        rem = jnp.where(here, pltpu.roll(tot, 128 - 8 * il_n + xs * il_n, 1), rem)
+        for q in range(2):
+            away = lax.rem(128 + (xs - q) * il_n - 2 * il_n * x, 128)
+            mean[q] = jnp.where(here, pltpu.roll(tot, away, 1), mean[q])
+    out_rem[...] = rem[:, :TYPES]
     for q in range(2):
-        pick = jnp.sum(jnp.where(row8 == 2 * x + q, red4_out, 0.0), axis=0, keepdims=True)
-        hs_pick = jnp.where(iota((2, 128), 0) == q, pick, hs_pick)
-    out_mean[...] = hs_pick[:, :TYPES]
+        out_mean[q:q + 1, :] = mean[q][:, :TYPES]
     for cp in sends:
         cp.wait_send()
 
@@ -314,7 +322,7 @@
     groups = ns * ny
     dims = (nz, ny, nc, nx, float(ncell * owned))
     any_, vm = pl.BlockSpec(memory_space=pl.ANY), pl.BlockSpec(memory_space=pltpu.VMEM)
-    sm = pl.BlockSpec(memory_space=pltpu.SMEM)
+    hbm = pl.BlockSpec(memory_space=pltpu.HBM)
     dma = pltpu.SemaphoreType.DMA
 
     def body(fractions, order, density, area, harvest):
@@ -340,17 +348,15 @@
             pltpu.VMEM((il_n, owned), F32),
             pltpu.VMEM((nx, 2, il_n, owned), F32),
             pltpu.VMEM((nx, il_n, owned), F32),
-            pltpu.VMEM((8, 128), F32),
-            pltpu.VMEM((ns, 8, 128), F32),
-            pltpu.VMEM((8, 128), F32),
-            pltpu.VMEM((ny, 8, 128), F32),
-            pltpu.VMEM((8, 128), F32),
-            pltpu.VMEM((nx, 8, 128), F32),
-            dma((5,)),
+            pltpu.VMEM((1, 128), F32),
+            pltpu.VMEM((ns, 1, 128), F32),
+            pltpu.VMEM((1, 128), F32),
+            pltpu.VMEM((ny * nx, 1, 128), F32),
+            dma((6,)),
         ]
-        for n in (nx, nx, ns, ns, ny, ny, nx, nx, ns, ny, nx):
+        for n in (nx, nx, ns, ns, ny, ny, nx, nx, ns, ny * nx):
             scratch += [dma((n,)), dma((n,))]
-        dens, cum, mean, rem = pl.pallas_call(
+        results = pl.pallas_call(
             functools.partial(kernel, dims),
             out_shape=(
                 jax.ShapeDtypeStruct((2, TYPES, owned), F32),
@@ -358,11 +364,19 @@
                 jax.ShapeDtypeStruct((2, TYPES), F32),
                 jax.ShapeDtypeStruct((1, TYPES), F32),
             ),
-            in_specs=[any_, any_, any_, any_, sm],
+            in_specs=[hbm] * 5,
             out_specs=(vm, vm, vm, vm),
             scratch_shapes=scratch,
-            compiler_params=pltpu.CompilerParams(collective_id=0, has_side_effects=True),
-        )(fractions, order.reshape(ny, 128), density, area, harvest)
+            compiler_params=pltpu.CompilerParams(collective_id=0, has_side_effects=True, vmem_limit_bytes=VMEM_LIMIT),
+        )(*(pltpu.with_memory_space_constraint(a, pltpu.HBM) for a in (fractions, order.reshape(ny, 128), density, area, harvest)))
+        dens, cum, mean, rem = pl.pallas_call(
+            hand_over,
+            out_shape=tuple(jax.ShapeDtypeStruct(r.shape, r.dtype) for r in results),
+            in_specs=[any_] * 4,
+            out_specs=(hbm,) * 4,
+            scratch_shapes=[dma((4,))],
+            compiler_params=pltpu.CompilerParams(vmem_limit_bytes=VMEM_LIMIT),
+        )(*results)
         return dens, cum, mean, rem.reshape(TYPES)
 
     cell = ("z", "y", "core")

time: 47.7 us -> 42.3 us (0.89)
  local copies, waits for them, and re-layouts: 3.4 us -> 0 us
  Pallas kernels: 43.4 us -> 41.5 us
    unnamed x10 -> x0, local copies, waits for them, and re-layouts: 3.4 us -> none
    pallas_call x1, Pallas kernels: 43.4 us -> 40.8 us  [body(): pl.pallas_call(functools.partial(kernel, dims), out_shape=(jax.ShapeDtype...]
    pallas_call x0 -> x1, Pallas kernels: none -> 0.71 us  [body(): pl.pallas_call(hand_over, out_shape=tuple((jax.ShapeDtypeStruct(r.shape,...]
where the time goes in v2:
time: 42.3 us; the launch traced here: 42.2 us
  Pallas kernels  41.5 us (98%)
  between operations  0.64 us (2%)
    pallas_call x1, Pallas kernels, body(): pl.pallas_call(functools.partial(kernel, dims), out_shape=(jax.ShapeDtype...  40.8 us

profile of v2, /device:TPU:1, one launch (start us, length us, event | category | flops | bytes accessed | tf_op | source)
XLA Modules:
  0.0 42.2 jit_solution(5436020644674601739)
XLA Ops:
  0.6 40.8 %shard_map.84 = (f32[2,16,1024]{2,1,0:T(8,128)S(1)}, f32[16,1024]{1,0:T(8,128)S(1)}, f32[2,16]{1,0:T(2,128)S(1)}, f32[1,16]{1,0:T(1,128)S(1)}) custom-call(bf16[256,1024]{1,0:T(8,128)(2,1)} %frac.1, s32[8,128]{1,0:T(8,128)} %bitcast.2, f32[2,16,1024]{2,1,0:T(8,128)} %dens.1, f32[16,1024]{1,0:T(8,128)} %area.1, f32[2]{0:T(128)} %harv.1), custom_call_target="tpu_custom_call" | custom-call | tf_op jit(solution)/shard_map/pallas_call | solution.py:359
  41.5 0.7 %shard_map.85 = (f32[2,16,1024]{2,1,0:T(8,128)}, f32[16,1024]{1,0:T(8,128)}, f32[2,16]{1,0:T(2,128)}, f32[1,16]{1,0:T(1,128)}) custom-call(f32[2,16,1024]{2,1,0:T(8,128)S(1)} %get-tuple-element.12.refs_0_, f32[16,1024]{1,0:T(8,128)S(1)} %get-tuple-element.13.refs_1_, f32[2,16]{1,0:T(2,128)S(1)} %get-tuple-element.14.refs_2_, ...), custom_call_target="tpu_custom_call" | custom-call | tf_op jit(solution)/shard_map/pallas_call | solution.py:372

commit v3 on v2

--- a/solution.py
+++ b/solution.py
@@ -32,9 +32,9 @@
 
 
 def kernel(dims, frac, order, dens, area, harv, out_dens, out_cum, out_mean, out_rem,
-           f2, ordv, areav, hsm, hs, hg, dg, stock, oh, psend, pa, ps2, pb, sd, av, bv,
+           f2, ordv, areav, hsm, hs, hg, dg, stock, sd, av, bv,
            mv, snd, snd_a, rcv, rcv_a, red0, red1, red2, red3, lsem,
-           d_s, d_r, h_s, h_r, p1_s, p1_r, s1_s, s1_r, p2_s, p2_r, s2_s, s2_r,
+           d_s, d_r, h_s, h_r, s1_s, s1_r, s2_s, s2_r,
            o_s, o_r, a_s, a_r, r1_s, r1_r, r2_s, r2_r):
     nz, ny, nc, nx, cells = dims
     ns = nz * nc
@@ -74,7 +74,8 @@
         cp.start()
 
     barrier = pltpu.get_barrier_semaphore()
-    peers = [dev_yx(o) for o in range(1, ny * nx)]
+    peers = [dev_x(o)[1] for o in range(1, nx)]
+    peers += [dev_y(o)[1] for o in range(1, ny)]
     peers += [dev_s(o)[1] for o in range(1, ns)]
     for p in peers:
         pl.semaphore_signal(barrier, inc=1, device_id=p, device_id_type=MESH)
@@ -93,7 +94,6 @@
     for b in range(ny):
         hot = iota((groups, 128), 0) == group[b:b + 1, :]
         hotb = hot.astype(BF16)
-        oh[:, b * 128:(b + 1) * 128] = hotb
         count = jnp.dot(hotb, upper, preferred_element_type=F32) + before
         if b < ny - 1:
             before = before + jnp.dot(hotb, ones, preferred_element_type=F32)
@@ -102,17 +102,20 @@
     part = rank // half_n
     sub = lax.rem(rank, half_n)
 
-    lane_of = part * (ns * half_n) + me * half_n + sub
+    home = dz * nc + dc
+    lane_of = part * 64 + lax.rem(me + dy, ns) * half_n + sub
     hi = (pos // 32).astype(F32)
     lo = lax.rem(pos, 32).astype(F32)
-    acc_hi = jnp.zeros((groups, 128), F32)
-    acc_lo = jnp.zeros((groups, 128), F32)
+    digit = lax.rem(iota((ns * half_n, 128), 0), half_n)
+    owner = iota((ns * half_n, 128), 0) // half_n
+    left, right = [], []
     for b in range(ny):
-        hot = oh[:, b * 128:(b + 1) * 128]
-        sel = iota((128, 128), 0) == lane_of[b:b + 1, :]
-        acc_hi += nt(hot, jnp.where(sel, hi[b:b + 1, :], 0.0).astype(BF16))
-        acc_lo += nt(hot, jnp.where(sel, lo[b:b + 1, :], 0.0).astype(BF16))
-    psend[...] = (acc_hi * 32.0 + acc_lo).reshape(ns, ny, 128)
+        r = slice(b, b + 1)
+        value = jnp.where(digit == 0, hi[r], jnp.where(digit == 1, lo[r], 0.0))
+        left.append(jnp.where(owner == home[r], value, 0.0).astype(BF16))
+        right.append((iota((128, 128), 0) == lane_of[r]).astype(BF16))
+    placed = nt(jnp.concatenate(left, axis=1), jnp.concatenate(right, axis=1))
+    sd[:, ny] = placed.astype(BF16).reshape(ns, half_n, 128)
 
     sends = []
 
@@ -140,17 +143,16 @@
         halves.append(nt(jnp.concatenate(hots, axis=1), f2[...]))
     lanes = iota((rho, 128), 1)
     moved_cols = jnp.where(lanes < rows, halves[0], halves[1]).astype(BF16)
-    sd[...] = moved_cols.reshape(ns, ny, half_n, 128)
+    sd[:, :ny] = moved_cols.reshape(ns, ny, half_n, 128)
 
     local[5].wait()
     row8, lane8 = iota((8, 128), 0), iota((8, 128), 1)
     hs[...] = jnp.where(row8 == 2 * x, hsm[0], jnp.where(row8 == 2 * x + 1, hsm[1], 0.0))
 
     pl.semaphore_wait(barrier, len(peers))
-    p1, s1 = [], []
+    s1 = []
     for o in far_s:
         t, to = dev_s(o)
-        p1.append(send(psend.at[t], pa.at[me], p1_s.at[o], p1_r.at[o], to))
         s1.append(send(sd.at[t], av.at[me], s1_s.at[o], s1_r.at[o], to))
     dcp, hcp = [], []
     for o in far_x:
@@ -158,28 +160,22 @@
         hcp.append(send(hs, hg.at[x], h_s.at[o], h_r.at[o], to))
         dcp.append(send(dens, dg.at[pl.ds(2 * x, 2)], d_s.at[o], d_r.at[o], to))
     av[pl.ds(me, 1)] = sd[pl.ds(me, 1)]
-    pa[pl.ds(me, 1)] = psend[pl.ds(me, 1)]
     hg[pl.ds(x, 1)] = hs[...].reshape(1, 8, 128)
 
-    for cp in p1:
-        cp.wait_recv()
-    ptot = pa[0]
-    for s in range(1, ns):
-        ptot = ptot + pa[s]
-    ps2[...] = ptot.reshape(ny, 1, 128)
-    p2 = []
-    for o in far_y:
-        t, to = dev_y(o)
-        p2.append(send(ps2.at[t], pb.at[slot[o]], p2_s.at[o], p2_r.at[o], to))
-    pb[0:1] = ps2[pl.ds(y, 1)]
-
-    for cp in s1:
-        cp.wait_recv()
+    shape3 = (ny, half_n, 128)
+    source = lax.rem(lax.rem(iota(shape3, 2), 64) // half_n + ns - iota(shape3, 0), ns)
+    placed = jnp.zeros(shape3, F32)
+    for o in [0] + far_s[::-1]:
+        src = lax.rem(me + ns - o, ns)
+        if o:
+            s1[far_s.index(o)].wait_recv()
+        placed = jnp.where(source == src, av[pl.ds(src, 1), ny].astype(F32), placed)
+    av[ns, :ny] = placed.astype(BF16)
     s2 = []
     for o in far_y:
         t, to = dev_y(o)
         s2.append(send(av.at[:, t], bv.at[slot[o]], s2_s.at[o], s2_r.at[o], to))
-    bv[0:1] = av[:, pl.ds(y, 1)].reshape(1, ns, half_n, 128)
+    bv[0:1] = av[:, pl.ds(y, 1)].reshape(1, ns + 1, half_n, 128)
 
     for cp in hcp:
         cp.wait_recv()
@@ -193,28 +189,24 @@
     for j in range(TYPES):
         stock[j] = dg[:, j, :] * areav[j:j + 1, :]
 
-    for cp in p2:
-        cp.wait_recv()
     low = iota((1, 128), 1) < 64
-    hots = [[], []]
+    same = lax.rem(iota((1, 128), 1), 64) < 64 - half_n * y
     for q in range(ny // 2):
-        a, b = pb[2 * q], pb[2 * q + 1]
-        ra, rb = pltpu.roll(a, 64, 1), pltpu.roll(b, 64, 1)
-        for h, v in enumerate((jnp.where(low, a, rb), jnp.where(low, ra, b))):
-            hots[h].append((iota((owned, 128), 0) == v.astype(I32)).astype(BF16))
-    spread = [jnp.concatenate(v, axis=1) for v in hots]
-
-    per = ny // 2
-    width = per * ns * half_n
-    for g in range(2):
-        for o, cp in zip(far_y, s2):
-            if slot[o] // per == g:
-                cp.wait_recv()
-        turned = bv[g * per:(g + 1) * per].reshape(width, 128).T
-        got = [nt(turned[h * rows:(h + 1) * rows], spread[h][:, g * width:(g + 1) * width]) for h in range(2)]
-        if g == 0:
-            near = got[0] + got[1]
-    mv[...] = near + (got[0] + got[1])
+        rolled = []
+        for k in (2 * q, 2 * q + 1):
+            for o, cp in zip(far_y, s2):
+                if slot[o] == k:
+                    cp.wait_recv()
+            digits = bv[k, ns].astype(F32)
+            p = digits[0:1] * 32.0 + digits[1:2]
+            rolled.append((pltpu.roll(p, 128 - half_n * y, 1), pltpu.roll(p, 64 - half_n * y, 1)))
+        (a1, a2), (b1, b2) = rolled
+        firsts = jnp.where(low, jnp.where(same, a1, a2), jnp.where(same, b2, b1)).astype(I32)
+        seconds = jnp.where(low, jnp.where(same, a2, a1), jnp.where(same, b1, b2)).astype(I32)
+        spread = jnp.concatenate([(iota((owned, 128), 0) == v).astype(BF16) for v in (firsts, seconds)], axis=1)
+        turned = bv[2 * q:2 * q + 2, :ns].reshape(128, 128).T
+        got = nt(jnp.concatenate([turned[:rows], turned[rows:]], axis=1), spread)
+        mv[...] = got if q == 0 else mv[...] + got
 
     keep = 1.0 - harvest
     zero = jnp.zeros((8, 128), F32)
@@ -243,12 +235,6 @@
     zeros = (zero,) * il_n
     sums, gone = lax.fori_loop(0, ny, block, (zeros, zeros))
 
-    ocp = []
-    for o in far_x:
-        t, to = dev_x(o)
-        ocp.append(send(snd_a, rcv_a.at[x], a_s.at[o], a_r.at[o], to))
-        ocp.append(send(snd.at[pl.ds(2 * t, 2)], rcv.at[x], o_s.at[o], o_r.at[o], to))
-
     word = zero
     for il in range(il_n):
         word = jnp.where(lane8 == row8 * il_n + il, jnp.sum(sums[il], axis=1, keepdims=True), word)
@@ -260,6 +246,12 @@
         t, to = dev_s(o)
         rc.append(send(red0, red1.at[me], r1_s.at[o], r1_r.at[o], to))
     red1[pl.ds(me, 1)] = word.reshape(1, 1, 128)
+    ocp = []
+    for o in far_x:
+        t, to = dev_x(o)
+        ocp.append(send(snd_a, rcv_a.at[x], a_s.at[o], a_r.at[o], to))
+        ocp.append(send(snd.at[pl.ds(2 * t, 2)], rcv.at[x], o_s.at[o], o_r.at[o], to))
+
     rcv[pl.ds(x, 1)] = snd[pl.ds(2 * x, 2)].reshape(1, 2, il_n, owned)
     rcv_a[pl.ds(x, 1)] = snd_a[...].reshape(1, il_n, owned)
     for cp in rc:
@@ -335,14 +327,9 @@
             pltpu.VMEM((nx, 8, 128), F32),
             pltpu.VMEM((2 * nx, TYPES, owned), F32),
             pltpu.VMEM((TYPES, 2 * nx, owned), F32),
-            pltpu.VMEM((groups, owned), BF16),
-            pltpu.VMEM((ns, ny, 128), F32),
-            pltpu.VMEM((ns, ny, 128), F32),
-            pltpu.VMEM((ny, 1, 128), F32),
-            pltpu.VMEM((ny, 1, 128), F32),
-            pltpu.VMEM((ns, ny, half_n, 128), BF16),
-            pltpu.VMEM((ns, ny, half_n, 128), BF16),
-            pltpu.VMEM((ny, ns, half_n, 128), BF16),
+            pltpu.VMEM((ns, ny + 1, half_n, 128), BF16),
+            pltpu.VMEM((ns + 1, ny + 1, half_n, 128), BF16),
+            pltpu.VMEM((ny, ns + 1, half_n, 128), BF16),
             pltpu.VMEM((rows, owned), F32),
             pltpu.VMEM((2 * nx, il_n, owned), F32),
             pltpu.VMEM((il_n, owned), F32),
@@ -354,7 +341,7 @@
             pltpu.VMEM((ny * nx, 1, 128), F32),
             dma((6,)),
         ]
-        for n in (nx, nx, ns, ns, ny, ny, nx, nx, ns, ny * nx):
+        for n in (nx, nx, ns, ny, nx, nx, ns, ny * nx):
             scratch += [dma((n,)), dma((n,))]
         results = pl.pallas_call(
             functools.partial(kernel, dims),

time: 42.3 us -> 41.6 us (0.983)
  Pallas kernels: 41.5 us -> 40.8 us
    pallas_call x1, Pallas kernels: 40.8 us -> 40.1 us  [body(): pl.pallas_call(functools.partial(kernel, dims), out_shape=(jax.ShapeDtype...]
where the time goes in v3:
time: 41.6 us; the launch traced here: 41.4 us
  Pallas kernels  40.8 us (98%)
  between operations  0.64 us (2%)
    pallas_call x1, Pallas kernels, body(): pl.pallas_call(functools.partial(kernel, dims), out_shape=(jax.ShapeDtype...  40.1 us

profile of v3, /device:TPU:1, one launch (start us, length us, event | category | flops | bytes accessed | tf_op | source)
XLA Modules:
  0.0 41.4 jit_solution(400686499103993041)
XLA Ops:
  0.6 40.1 %shard_map.84 = (f32[2,16,1024]{2,1,0:T(8,128)S(1)}, f32[16,1024]{1,0:T(8,128)S(1)}, f32[2,16]{1,0:T(2,128)S(1)}, f32[1,16]{1,0:T(1,128)S(1)}) custom-call(bf16[256,1024]{1,0:T(8,128)(2,1)} %frac.1, s32[8,128]{1,0:T(8,128)} %bitcast.2, f32[2,16,1024]{2,1,0:T(8,128)} %dens.1, f32[16,1024]{1,0:T(8,128)} %area.1, f32[2]{0:T(128)} %harv.1), custom_call_target="tpu_custom_call" | custom-call | tf_op jit(solution)/shard_map/pallas_call | solution.py:346
  40.7 0.7 %shard_map.85 = (f32[2,16,1024]{2,1,0:T(8,128)}, f32[16,1024]{1,0:T(8,128)}, f32[2,16]{1,0:T(2,128)}, f32[1,16]{1,0:T(1,128)}) custom-call(f32[2,16,1024]{2,1,0:T(8,128)S(1)} %get-tuple-element.12.refs_0_, f32[16,1024]{1,0:T(8,128)S(1)} %get-tuple-element.13.refs_1_, f32[2,16]{1,0:T(2,128)S(1)} %get-tuple-element.14.refs_2_, ...), custom_call_target="tpu_custom_call" | custom-call | tf_op jit(solution)/shard_map/pallas_call | solution.py:359

commit v4 on v3

--- a/solution.py
+++ b/solution.py
@@ -104,8 +104,8 @@
 
     home = dz * nc + dc
     lane_of = part * 64 + lax.rem(me + dy, ns) * half_n + sub
-    hi = (pos // 32).astype(F32)
-    lo = lax.rem(pos, 32).astype(F32)
+    hi = (pos // 128).astype(F32)
+    lo = lax.rem(pos, 128).astype(F32)
     digit = lax.rem(iota((ns * half_n, 128), 0), half_n)
     owner = iota((ns * half_n, 128), 0) // half_n
     left, right = [], []
@@ -153,13 +153,13 @@
     s1 = []
     for o in far_s:
         t, to = dev_s(o)
-        s1.append(send(sd.at[t], av.at[me], s1_s.at[o], s1_r.at[o], to))
+        s1.append(send(sd.at[t], av.at[:, me], s1_s.at[o], s1_r.at[o], to))
     dcp, hcp = [], []
     for o in far_x:
         t, to = dev_x(o)
         hcp.append(send(hs, hg.at[x], h_s.at[o], h_r.at[o], to))
         dcp.append(send(dens, dg.at[pl.ds(2 * x, 2)], d_s.at[o], d_r.at[o], to))
-    av[pl.ds(me, 1)] = sd[pl.ds(me, 1)]
+    av[:, pl.ds(me, 1)] = sd[pl.ds(me, 1)].reshape(ny + 1, 1, half_n, 128)
     hg[pl.ds(x, 1)] = hs[...].reshape(1, 8, 128)
 
     shape3 = (ny, half_n, 128)
@@ -169,13 +169,13 @@
         src = lax.rem(me + ns - o, ns)
         if o:
             s1[far_s.index(o)].wait_recv()
-        placed = jnp.where(source == src, av[pl.ds(src, 1), ny].astype(F32), placed)
-    av[ns, :ny] = placed.astype(BF16)
+        placed = jnp.where(source == src, av[ny, pl.ds(src, 1)].astype(F32), placed)
+    av[:ny, ns] = placed.astype(BF16)
     s2 = []
     for o in far_y:
         t, to = dev_y(o)
-        s2.append(send(av.at[:, t], bv.at[slot[o]], s2_s.at[o], s2_r.at[o], to))
-    bv[0:1] = av[:, pl.ds(y, 1)].reshape(1, ns + 1, half_n, 128)
+        s2.append(send(av.at[t], bv.at[slot[o]], s2_s.at[o], s2_r.at[o], to))
+    bv[0:1] = av[pl.ds(y, 1)]
 
     for cp in hcp:
         cp.wait_recv()
@@ -189,23 +189,26 @@
     for j in range(TYPES):
         stock[j] = dg[:, j, :] * areav[j:j + 1, :]
 
-    low = iota((1, 128), 1) < 64
-    same = lax.rem(iota((1, 128), 1), 64) < 64 - half_n * y
+    low = iota((2, 128), 1) < 64
+    same = lax.rem(iota((2, 128), 1), 64) < 64 - half_n * y
     for q in range(ny // 2):
         rolled = []
         for k in (2 * q, 2 * q + 1):
             for o, cp in zip(far_y, s2):
                 if slot[o] == k:
                     cp.wait_recv()
-            digits = bv[k, ns].astype(F32)
-            p = digits[0:1] * 32.0 + digits[1:2]
-            rolled.append((pltpu.roll(p, 128 - half_n * y, 1), pltpu.roll(p, 64 - half_n * y, 1)))
+            digits = bv[k, ns].astype(F32)[0:2]
+            rolled.append((pltpu.roll(digits, 128 - half_n * y, 1), pltpu.roll(digits, 64 - half_n * y, 1)))
         (a1, a2), (b1, b2) = rolled
-        firsts = jnp.where(low, jnp.where(same, a1, a2), jnp.where(same, b2, b1)).astype(I32)
-        seconds = jnp.where(low, jnp.where(same, a2, a1), jnp.where(same, b1, b2)).astype(I32)
-        spread = jnp.concatenate([(iota((owned, 128), 0) == v).astype(BF16) for v in (firsts, seconds)], axis=1)
+        firsts = jnp.where(low, jnp.where(same, a1, a2), jnp.where(same, b2, b1))
+        seconds = jnp.where(low, jnp.where(same, a2, a1), jnp.where(same, b1, b2))
+        place = jnp.concatenate([firsts, seconds], axis=1).astype(I32)
+        spread = (iota((128, 256), 0) == place[1:2]).astype(BF16)
         turned = bv[2 * q:2 * q + 2, :ns].reshape(128, 128).T
-        got = nt(jnp.concatenate([turned[:rows], turned[rows:]], axis=1), spread)
+        turned = jnp.concatenate([turned[:rows], turned[rows:]], axis=1)
+        masks = (iota((ny, 256), 0) == place[0:1]).astype(BF16)
+        masked = jnp.concatenate([turned * masks[b:b + 1] for b in range(ny)], axis=0)
+        got = nt(masked, spread).reshape(ny, rows, 128)
         mv[...] = got if q == 0 else mv[...] + got
 
     keep = 1.0 - harvest
@@ -218,7 +221,7 @@
         for il in range(il_n):
             tot, na, stay = zero, zero, zero
             for j in range(TYPES):
-                m = jnp.broadcast_to(mv[il * TYPES + j:il * TYPES + j + 1, cols], (8, 128))
+                m = jnp.broadcast_to(mv[lb, il * TYPES + j:il * TYPES + j + 1, :], (8, 128))
                 term = m * stock[j, :, cols]
                 tot = tot + term
                 if j % il_n == il:
@@ -328,9 +331,9 @@
             pltpu.VMEM((2 * nx, TYPES, owned), F32),
             pltpu.VMEM((TYPES, 2 * nx, owned), F32),
             pltpu.VMEM((ns, ny + 1, half_n, 128), BF16),
-            pltpu.VMEM((ns + 1, ny + 1, half_n, 128), BF16),
+            pltpu.VMEM((ny + 1, ns + 1, half_n, 128), BF16),
             pltpu.VMEM((ny, ns + 1, half_n, 128), BF16),
-            pltpu.VMEM((rows, owned), F32),
+            pltpu.VMEM((ny, rows, 128), F32),
             pltpu.VMEM((2 * nx, il_n, owned), F32),
             pltpu.VMEM((il_n, owned), F32),
             pltpu.VMEM((nx, 2, il_n, owned), F32),

time: 41.6 us -> 41.3 us (level)
  no operation moved by 1% of the time
where the time goes in v4:
time: 41.3 us; the launch traced here: 41.2 us
  Pallas kernels  40.5 us (98%)
  between operations  0.64 us (2%)
    pallas_call x1, Pallas kernels, body(): pl.pallas_call(functools.partial(kernel, dims), out_shape=(jax.ShapeDtype...  39.8 us

profile of v4, /device:TPU:1, one launch (start us, length us, event | category | flops | bytes accessed | tf_op | source)
XLA Modules:
  0.0 41.2 jit_solution(15208363663927532161)
XLA Ops:
  0.6 39.8 %shard_map.84 = (f32[2,16,1024]{2,1,0:T(8,128)S(1)}, f32[16,1024]{1,0:T(8,128)S(1)}, f32[2,16]{1,0:T(2,128)S(1)}, f32[1,16]{1,0:T(1,128)S(1)}) custom-call(bf16[256,1024]{1,0:T(8,128)(2,1)} %frac.1, s32[8,128]{1,0:T(8,128)} %bitcast.2, f32[2,16,1024]{2,1,0:T(8,128)} %dens.1, f32[16,1024]{1,0:T(8,128)} %area.1, f32[2]{0:T(128)} %harv.1), custom_call_target="tpu_custom_call" | custom-call | tf_op jit(solution)/shard_map/pallas_call | solution.py:349
  40.4 0.7 %shard_map.85 = (f32[2,16,1024]{2,1,0:T(8,128)}, f32[16,1024]{1,0:T(8,128)}, f32[2,16]{1,0:T(2,128)}, f32[1,16]{1,0:T(1,128)}) custom-call(f32[2,16,1024]{2,1,0:T(8,128)S(1)} %get-tuple-element.12.refs_0_, f32[16,1024]{1,0:T(8,128)S(1)} %get-tuple-element.13.refs_1_, f32[2,16]{1,0:T(2,128)S(1)} %get-tuple-element.14.refs_2_, ...), custom_call_target="tpu_custom_call" | custom-call | tf_op jit(solution)/shard_map/pallas_call | solution.py:362

commit v5 on v4

--- a/solution.py
+++ b/solution.py
@@ -129,7 +129,8 @@
     far_s = sorted(range(1, ns), key=lambda o: -min(o, ns - o))
     far_y = sorted(range(1, ny), key=lambda o: -min(o, ny - o))
     far_yx = sorted(range(1, ny * nx), key=lambda o: -min(o // nx, ny - o // nx) - min(o % nx, nx - o % nx))
-    slot = {o: ny - 1 - far_y.index(o) for o in far_y}
+    near_y = far_y[::-1]
+    slot = {o: 1 + near_y.index(o) for o in near_y}
     far_x = sorted(range(1, nx), key=lambda o: -min(o, nx - o))
 
     key = group * half_n + sub
@@ -172,7 +173,7 @@
         placed = jnp.where(source == src, av[ny, pl.ds(src, 1)].astype(F32), placed)
     av[:ny, ns] = placed.astype(BF16)
     s2 = []
-    for o in far_y:
+    for o in near_y:
         t, to = dev_y(o)
         s2.append(send(av.at[t], bv.at[slot[o]], s2_s.at[o], s2_r.at[o], to))
     bv[0:1] = av[pl.ds(y, 1)]
@@ -194,7 +195,7 @@
     for q in range(ny // 2):
         rolled = []
         for k in (2 * q, 2 * q + 1):
-            for o, cp in zip(far_y, s2):
+            for o, cp in zip(near_y, s2):
                 if slot[o] == k:
                     cp.wait_recv()
             digits = bv[k, ns].astype(F32)[0:2]

time: 41.3 us -> 40.7 us (0.985)
  Pallas kernels: 40.5 us -> 39.9 us
    pallas_call x1, Pallas kernels: 39.8 us -> 39.2 us  [body(): pl.pallas_call(functools.partial(kernel, dims), out_shape=(jax.ShapeDtype...]
where the time goes in v5:
time: 40.7 us; the launch traced here: 40.6 us
  Pallas kernels  39.9 us (98%)
  between operations  0.64 us (2%)
    pallas_call x1, Pallas kernels, body(): pl.pallas_call(functools.partial(kernel, dims), out_shape=(jax.ShapeDtype...  39.2 us

profile of v5, /device:TPU:1, one launch (start us, length us, event | category | flops | bytes accessed | tf_op | source)
XLA Modules:
  0.0 40.6 jit_solution(11494722330973213771)
XLA Ops:
  0.6 39.2 %shard_map.84 = (f32[2,16,1024]{2,1,0:T(8,128)S(1)}, f32[16,1024]{1,0:T(8,128)S(1)}, f32[2,16]{1,0:T(2,128)S(1)}, f32[1,16]{1,0:T(1,128)S(1)}) custom-call(bf16[256,1024]{1,0:T(8,128)(2,1)} %frac.1, s32[8,128]{1,0:T(8,128)} %bitcast.2, f32[2,16,1024]{2,1,0:T(8,128)} %dens.1, f32[16,1024]{1,0:T(8,128)} %area.1, f32[2]{0:T(128)} %harv.1), custom_call_target="tpu_custom_call" | custom-call | tf_op jit(solution)/shard_map/pallas_call | solution.py:350
  39.8 0.7 %shard_map.85 = (f32[2,16,1024]{2,1,0:T(8,128)}, f32[16,1024]{1,0:T(8,128)}, f32[2,16]{1,0:T(2,128)}, f32[1,16]{1,0:T(1,128)}) custom-call(f32[2,16,1024]{2,1,0:T(8,128)S(1)} %get-tuple-element.12.refs_0_, f32[16,1024]{1,0:T(8,128)S(1)} %get-tuple-element.13.refs_1_, f32[2,16]{1,0:T(2,128)S(1)} %get-tuple-element.14.refs_2_, ...), custom_call_target="tpu_custom_call" | custom-call | tf_op jit(solution)/shard_map/pallas_call | solution.py:363

commit v6 on v5

--- a/solution.py
+++ b/solution.py
@@ -18,6 +18,14 @@
     return lax.dot_general(a, b, (((1,), (1,)), ((), ())), preferred_element_type=F32)
 
 
+def nearness(o, n):
+    return jnp.where(2 * o < n, jnp.maximum(2 * o - 1, 0), jnp.where(2 * o == n, n - 1, 2 * (n - o)))
+
+
+def near_slot(o, n):
+    return max(2 * o - 1, 0) if 2 * o < n else n - 1 if 2 * o == n else 2 * (n - o)
+
+
 def iota(shape, dim):
     return lax.broadcasted_iota(I32, shape, dim)
 
@@ -34,7 +42,7 @@
 def kernel(dims, frac, order, dens, area, harv, out_dens, out_cum, out_mean, out_rem,
            f2, ordv, areav, hsm, hs, hg, dg, stock, sd, av, bv,
            mv, snd, snd_a, rcv, rcv_a, red0, red1, red2, red3, lsem,
-           d_s, d_r, h_s, h_r, s1_s, s1_r, s2_s, s2_r,
+           d_s, d_r, h_s, h_r, s1_s, s1_r, s2_s, s2_r, s2a_s, s2a_r,
            o_s, o_r, a_s, a_r, r1_s, r1_r, r2_s, r2_r):
     nz, ny, nc, nx, cells = dims
     ns = nz * nc
@@ -74,9 +82,9 @@
         cp.start()
 
     barrier = pltpu.get_barrier_semaphore()
-    peers = [dev_x(o)[1] for o in range(1, nx)]
-    peers += [dev_y(o)[1] for o in range(1, ny)]
-    peers += [dev_s(o)[1] for o in range(1, ns)]
+    peers = [dev_s(o)[1] for o in sorted(range(1, ns), key=lambda o: -min(o, ns - o))]
+    peers += [dev_y(o)[1] for o in sorted(range(1, ny), key=lambda o: -min(o, ny - o))]
+    peers += [dev_x(o)[1] for o in range(1, nx)]
     for p in peers:
         pl.semaphore_signal(barrier, inc=1, device_id=p, device_id_type=MESH)
 
@@ -103,7 +111,7 @@
     sub = lax.rem(rank, half_n)
 
     home = dz * nc + dc
-    lane_of = part * 64 + lax.rem(me + dy, ns) * half_n + sub
+    lane_of = part * 64 + lax.rem(nearness(lax.rem(home + ns - me, ns), ns) + dy, ns) * half_n + sub
     hi = (pos // 128).astype(F32)
     lo = lax.rem(pos, 128).astype(F32)
     digit = lax.rem(iota((ns * half_n, 128), 0), half_n)
@@ -152,30 +160,34 @@
 
     pl.semaphore_wait(barrier, len(peers))
     s1 = []
-    for o in far_s:
+    for o in far_s[::-1]:
         t, to = dev_s(o)
-        s1.append(send(sd.at[t], av.at[:, me], s1_s.at[o], s1_r.at[o], to))
+        s1.append(send(sd.at[t], av.at[:, near_slot(o, ns)], s1_s.at[o], s1_r.at[o], to))
+    s1 = s1[::-1]
     dcp, hcp = [], []
     for o in far_x:
         t, to = dev_x(o)
         hcp.append(send(hs, hg.at[x], h_s.at[o], h_r.at[o], to))
         dcp.append(send(dens, dg.at[pl.ds(2 * x, 2)], d_s.at[o], d_r.at[o], to))
-    av[:, pl.ds(me, 1)] = sd[pl.ds(me, 1)].reshape(ny + 1, 1, half_n, 128)
+    av[:, 0:1] = sd[pl.ds(me, 1)].reshape(ny + 1, 1, half_n, 128)
     hg[pl.ds(x, 1)] = hs[...].reshape(1, 8, 128)
 
     shape3 = (ny, half_n, 128)
     source = lax.rem(lax.rem(iota(shape3, 2), 64) // half_n + ns - iota(shape3, 0), ns)
     placed = jnp.zeros(shape3, F32)
-    for o in [0] + far_s[::-1]:
-        src = lax.rem(me + ns - o, ns)
+    first, s2a, s2 = ns // 2, [], []
+    for k, o in enumerate(sorted(range(ns), key=lambda o: near_slot(o, ns))):
         if o:
             s1[far_s.index(o)].wait_recv()
-        placed = jnp.where(source == src, av[ny, pl.ds(src, 1)].astype(F32), placed)
+        placed = jnp.where(source == k, av[ny, k:k + 1].astype(F32), placed)
+        if k == first - 1:
+            for p in near_y:
+                t, to = dev_y(p)
+                s2a.append(send(av.at[t, pl.ds(0, first)], bv.at[slot[p], pl.ds(0, first)], s2a_s.at[p], s2a_r.at[p], to))
     av[:ny, ns] = placed.astype(BF16)
-    s2 = []
     for o in near_y:
         t, to = dev_y(o)
-        s2.append(send(av.at[t], bv.at[slot[o]], s2_s.at[o], s2_r.at[o], to))
+        s2.append(send(av.at[t, pl.ds(first, ns + 1 - first)], bv.at[slot[o], pl.ds(first, ns + 1 - first)], s2_s.at[o], s2_r.at[o], to))
     bv[0:1] = av[pl.ds(y, 1)]
 
     for cp in hcp:
@@ -195,8 +207,9 @@
     for q in range(ny // 2):
         rolled = []
         for k in (2 * q, 2 * q + 1):
-            for o, cp in zip(near_y, s2):
+            for o, ca, cp in zip(near_y, s2a, s2):
                 if slot[o] == k:
+                    ca.wait_recv()
                     cp.wait_recv()
             digits = bv[k, ns].astype(F32)[0:2]
             rolled.append((pltpu.roll(digits, 128 - half_n * y, 1), pltpu.roll(digits, 64 - half_n * y, 1)))
@@ -345,7 +358,7 @@
             pltpu.VMEM((ny * nx, 1, 128), F32),
             dma((6,)),
         ]
-        for n in (nx, nx, ns, ny, nx, nx, ns, ny * nx):
+        for n in (nx, nx, ns, ny, ny, nx, nx, ns, ny * nx):
             scratch += [dma((n,)), dma((n,))]
         results = pl.pallas_call(
             functools.partial(kernel, dims),

time: 40.7 us -> 40.3 us (level)
  no operation moved by 1% of the time
where the time goes in v6:
time: 40.3 us; the launch traced here: 40.2 us
  Pallas kernels  39.5 us (98%)
  between operations  0.64 us (2%)
    pallas_call x1, Pallas kernels, body(): pl.pallas_call(functools.partial(kernel, dims), out_shape=(jax.ShapeDtype...  38.8 us

profile of v6, /device:TPU:1, one launch (start us, length us, event | category | flops | bytes accessed | tf_op | source)
XLA Modules:
  0.0 40.2 jit_solution(16800989181736387923)
XLA Ops:
  0.6 38.8 %shard_map.84 = (f32[2,16,1024]{2,1,0:T(8,128)S(1)}, f32[16,1024]{1,0:T(8,128)S(1)}, f32[2,16]{1,0:T(2,128)S(1)}, f32[1,16]{1,0:T(1,128)S(1)}) custom-call(bf16[256,1024]{1,0:T(8,128)(2,1)} %frac.1, s32[8,128]{1,0:T(8,128)} %bitcast.2, f32[2,16,1024]{2,1,0:T(8,128)} %dens.1, f32[16,1024]{1,0:T(8,128)} %area.1, f32[2]{0:T(128)} %harv.1), custom_call_target="tpu_custom_call" | custom-call | tf_op jit(solution)/shard_map/pallas_call | solution.py:363
  39.4 0.7 %shard_map.85 = (f32[2,16,1024]{2,1,0:T(8,128)}, f32[16,1024]{1,0:T(8,128)}, f32[2,16]{1,0:T(2,128)}, f32[1,16]{1,0:T(1,128)}) custom-call(f32[2,16,1024]{2,1,0:T(8,128)S(1)} %get-tuple-element.12.refs_0_, f32[16,1024]{1,0:T(8,128)S(1)} %get-tuple-element.13.refs_1_, f32[2,16]{1,0:T(2,128)S(1)} %get-tuple-element.14.refs_2_, ...), custom_call_target="tpu_custom_call" | custom-call | tf_op jit(solution)/shard_map/pallas_call | solution.py:376

commit v7 on v6

--- a/solution.py
+++ b/solution.py
@@ -259,7 +259,7 @@
     word = jnp.sum(word, axis=0, keepdims=True)
     red0[...] = word
     rc = []
-    for o in far_s:
+    for o in far_s[::-1]:
         t, to = dev_s(o)
         rc.append(send(red0, red1.at[me], r1_s.at[o], r1_r.at[o], to))
     red1[pl.ds(me, 1)] = word.reshape(1, 1, 128)
@@ -278,7 +278,7 @@
         tot = tot + red1[s]
     red2[...] = tot
     rc = []
-    for o in far_yx:
+    for o in far_yx[::-1]:
         to = dev_yx(o)
         rc.append(send(red2, red3.at[y * nx + x], r2_s.at[o], r2_r.at[o], to))
     red3[pl.ds(y * nx + x, 1)] = tot.reshape(1, 1, 128)

time: 40.3 us -> 40.4 us (level)
  no operation moved by 1% of the time
where the time goes in v7:
time: 40.4 us; the launch traced here: 40.3 us
  Pallas kernels  39.6 us (98%)
  between operations  0.64 us (2%)
    pallas_call x1, Pallas kernels, body(): pl.pallas_call(functools.partial(kernel, dims), out_shape=(jax.ShapeDtype...  38.9 us

profile of v7, /device:TPU:1, one launch (start us, length us, event | category | flops | bytes accessed | tf_op | source)
XLA Modules:
  0.0 40.3 jit_solution(14054954918197608983)
XLA Ops:
  0.6 38.9 %shard_map.84 = (f32[2,16,1024]{2,1,0:T(8,128)S(1)}, f32[16,1024]{1,0:T(8,128)S(1)}, f32[2,16]{1,0:T(2,128)S(1)}, f32[1,16]{1,0:T(1,128)S(1)}) custom-call(bf16[256,1024]{1,0:T(8,128)(2,1)} %frac.1, s32[8,128]{1,0:T(8,128)} %bitcast.2, f32[2,16,1024]{2,1,0:T(8,128)} %dens.1, f32[16,1024]{1,0:T(8,128)} %area.1, f32[2]{0:T(128)} %harv.1), custom_call_target="tpu_custom_call" | custom-call | tf_op jit(solution)/shard_map/pallas_call | solution.py:363
  39.6 0.7 %shard_map.85 = (f32[2,16,1024]{2,1,0:T(8,128)}, f32[16,1024]{1,0:T(8,128)}, f32[2,16]{1,0:T(2,128)}, f32[1,16]{1,0:T(1,128)}) custom-call(f32[2,16,1024]{2,1,0:T(8,128)S(1)} %get-tuple-element.12.refs_0_, f32[16,1024]{1,0:T(8,128)S(1)} %get-tuple-element.13.refs_1_, f32[2,16]{1,0:T(2,128)S(1)} %get-tuple-element.14.refs_2_, ...), custom_call_target="tpu_custom_call" | custom-call | tf_op jit(solution)/shard_map/pallas_call | solution.py:376
